TPU v7x, 256 devices: a whole 4x4x8 slice. The times are simulated.
256 devices in a mesh: dp: 32 (over x, z), tensor: 8 (over y, core).
Axes of the slice: x: 4, y: 4, z: 8, core: 2. Of those that a mesh axis runs over, the one named last changes fastest.
Arguments:
- tubelets: bfloat16 [1024, 32, 4096], P('dp', 'tensor'), may hold values from -6 to 6
- keep_index: int32 [1024, 32], P('dp', 'tensor'), may hold values from -1 to 31, as said below
- dest_row: int32 [1024, 32], P('dp', 'tensor'), may hold values from -1 to 31, as said below
- dest_slot: int32 [1024, 32], P('dp', 'tensor'), may hold values from -1 to 1023, as said below
- segment: int32 [32, 1024], P('dp'), may hold values from -1 to 1023, as said below
- ln_gain: bfloat16 [4096], replicated, may hold values from 0.25 to 1.75
- w_query: bfloat16 [4096, 3072], P('dp', 'tensor')
- w_key: bfloat16 [4096, 3072], P('dp', 'tensor')
- w_value: bfloat16 [4096, 3072], P('dp', 'tensor'), may hold values from -0.09375 to 0.09375
Outputs:
- attended: bfloat16 [32, 1024, 3072], P('dp', None, 'tensor')
Inputs may be any that keep to these rules, and one draw needn't show every extreme that they name: `keep_index`: entry e of a clip's list belongs to tensor index e // 4 and, when kept, names a tubelet of that index's share, each at most once; -1 marks a dropped entry. Each share keeps 1 to 4 tubelets. `dest_row`: -1 exactly where keep_index is -1. A clip goes whole to one row; each row receives exactly one clip from each dp index, so at most 4 kept tubelets go from one device to one row; some dp index sends that many to every row. `dest_slot`: -1 exactly where keep_index is -1. A kept tubelet on tensor index j lands in slots j * 128 to (j + 1) * 128 - 1; no two kept tubelets share a row and a slot; some row has all its slots filled. `segment`: the clip whose tubelet fills each slot, clips numbered in the order of the tubelets array; -1 for an empty slot. Agrees with dest_row and dest_slot.
All inputs are finite; a program needn't handle non-finite values.
Results may differ from a plain program's by a relative error of at most 0.0082.
Values may be sent and summed in bfloat16 or wider, within the bound.
A program may use at most 64 MiB of HBM per device.

v0:
```python
import jax
import jax.numpy as jnp
from jax import lax
from jax.sharding import PartitionSpec as P

HS = 128
block_rows = 512


def layer_norm(values_in, ln_gain):
    floats = values_in.astype(jnp.float32)
    average = jnp.mean(floats, axis=-1, keepdims=True)
    centred = floats - average
    variance = jnp.mean(centred * centred, axis=-1, keepdims=True)
    return (centred * lax.rsqrt(variance + 1e-06) * ln_gain.astype(jnp.float32)).astype(
        jnp.bfloat16
    )


def bucket_targets(row_ids, is_kept, n_buckets, capacity):
    matches = (row_ids[:, None] == jnp.arange(n_buckets, dtype=jnp.int32)[None, :]).astype(
        jnp.int32
    )
    earlier = jnp.cumsum(matches, axis=0) - matches
    ranking = jnp.sum(earlier * matches, axis=1)
    return jnp.where(is_kept, row_ids * capacity + ranking, -1)


def invert(targets, first_vals, second_vals, count):
    matches = targets[None, :] == jnp.arange(count, dtype=jnp.int32)[:, None]
    present = jnp.any(matches, axis=1)
    first_pick = jnp.sum(jnp.where(matches, first_vals[None, :], 0), axis=1)
    second_pick = jnp.sum(jnp.where(matches, second_vals[None, :], 0), axis=1)
    return (present, first_pick, second_pick)


def pack_send(flat_rows, source_ids, row_ids, slot_ids, is_kept, n_buckets):
    entries = source_ids.shape[0]
    capacity = entries // n_buckets
    targets = bucket_targets(row_ids, is_kept, n_buckets, capacity)
    present, source_pick, slot_pick = invert(targets, source_ids, slot_ids, entries)
    send_rows = jnp.where(
        present[:, None], jnp.take(flat_rows, source_pick, axis=0), jnp.zeros((), flat_rows.dtype)
    )
    send_slots = jnp.where(present, slot_pick, -1)
    return (
        send_rows.reshape(n_buckets, capacity, flat_rows.shape[1]),
        send_slots.reshape(n_buckets, capacity),
    )


def place_rows(recv_rows, recv_slots, slot_count):
    flat_rows = recv_rows.reshape(-1, recv_rows.shape[-1])
    flat_slots = recv_slots.reshape(-1)
    positions = jnp.arange(flat_slots.shape[0], dtype=jnp.int32)
    present, picked, ignored = invert(flat_slots, positions, positions, slot_count)
    return jnp.where(
        present[:, None], jnp.take(flat_rows, picked, axis=0), jnp.zeros((), flat_rows.dtype)
    )


def attend(query_rows, key_rows, value_rows, seg_query, seg_key):
    scores = jnp.einsum("qhd,khd->hqk", query_rows, key_rows, preferred_element_type=jnp.float32)
    allowed = (seg_query[:, None] == seg_key[None, :]) & (seg_key[None, :] >= 0)
    masked = jnp.where(allowed[None], scores, -1e30)
    largest = jnp.max(masked, axis=-1, keepdims=True)
    weights = jnp.where(allowed[None], jnp.exp(masked - largest), 0.0)
    totals = jnp.sum(weights, axis=-1, keepdims=True)
    totals = jnp.where(totals > 0, totals, 1.0)
    weights_bf = (weights / totals).astype(jnp.bfloat16)
    mixed = jnp.einsum("hqk,khd->qhd", weights_bf, value_rows, preferred_element_type=jnp.float32)
    return mixed.astype(jnp.bfloat16)


def body(tubelets, keep_index, dest_row, dest_slot, segment, ln_gain, w_query, w_key, w_value):
    n_rows = lax.axis_size("dp")
    clip_count, share_len, width = tubelets.shape
    seg_ids = segment.reshape(-1)
    row_len = seg_ids.shape[0]
    tok_rows = row_len // lax.axis_size("tensor")
    width_cols = w_query.shape[1]
    heads_local = width_cols // HS
    column = lax.axis_index("tensor")
    is_kept = (keep_index >= 0).reshape(-1)
    local_ids = jnp.maximum(keep_index - column * share_len, 0)
    source_ids = (jnp.arange(clip_count, dtype=jnp.int32)[:, None] * share_len + local_ids).reshape(
        -1
    )
    local_slots = (dest_slot - column * tok_rows).reshape(-1)
    send_rows, send_slots = pack_send(
        tubelets.reshape(-1, width), source_ids, dest_row.reshape(-1), local_slots, is_kept, n_rows
    )
    recv_rows, recv_slots = (
        lax.all_to_all(send_rows, "dp", split_axis=0, concat_axis=0, tiled=True),
        lax.all_to_all(send_slots, "dp", split_axis=0, concat_axis=0, tiled=True),
    )
    normed_own = layer_norm(place_rows(recv_rows, recv_slots, tok_rows), ln_gain)
    normed_row = lax.all_gather(normed_own, "tensor", axis=0, tiled=True)
    pieces_in = (
        lax.all_gather(w_query, "dp", axis=0, tiled=True),
        lax.all_gather(w_key, "dp", axis=0, tiled=True),
        lax.all_gather(w_value, "dp", axis=0, tiled=True),
    )
    query_sum, key_sum, value_sum = tuple(
        (jnp.dot(normed_row, piece_w, preferred_element_type=jnp.float32) for piece_w in pieces_in)
    )
    query_rows = (query_sum * HS ** (-0.5)).astype(jnp.bfloat16)
    key_rows = key_sum.astype(jnp.bfloat16).reshape(row_len, heads_local, HS)
    value_rows = value_sum.astype(jnp.bfloat16).reshape(row_len, heads_local, HS)
    blocks = row_len // block_rows
    query_blocks = query_rows.reshape(blocks, block_rows, heads_local, HS)
    seg_blocks = seg_ids.reshape(blocks, block_rows)
    mixed = lax.map(
        lambda pair_in: attend(pair_in[0], key_rows, value_rows, pair_in[1], seg_ids),
        (query_blocks, seg_blocks),
    )
    return mixed.reshape(1, row_len, width_cols)


def solution(mesh):
    return jax.shard_map(
        body,
        mesh=mesh,
        in_specs=(
            P("dp", "tensor", None),
            P("dp", "tensor"),
            P("dp", "tensor"),
            P("dp", "tensor"),
            P("dp", None),
            P(),
            P("dp", "tensor"),
            P("dp", "tensor"),
            P("dp", "tensor"),
        ),
        out_specs=P("dp", None, "tensor"),
        check_vma=False,
    )
```

profile of v0, /device:TPU:8, one launch (start us, length us, event | category | flops | bytes accessed | tf_op | source)
XLA Modules:
  0.0 343.9 jit_solution(8539267349982979860)
XLA Ops:
  6.5 0.7 all-gather.7.cloned.1.call-update
  7.3 0.8 copy.40
  8.0 0.1 reshape.153
  8.1 0.1 fusion.35
  8.2 0.7 broadcast_compare_fusion.1
  8.9 0.2 reduce_window_sum.11
  9.1 0.7 maximum_add_fusion
  9.8 0.7 broadcast_subtract_fusion
  10.5 0.2 select_reduce_fusion.4
  10.6 0.1 copy.39
  10.7 0.1 reshape.152
  10.9 0.1 copy.43
  11.0 0.1 broadcast_in_dim.112
  11.1 0.1 copy.41
  11.2 0.1 broadcast_in_dim.107
  11.3 0.1 fusion.34
  11.4 0.1 select_reduce_fusion.3
  11.5 0.7 select_n.65
  12.2 11.3 %all-to-all-start = ((s32[32,1,4]{2,1,0:T(1,128)}), s32[32,1,4]{2,1,0:T(1,128)S(1)}, u32[]{:S(2)}, u32[]{:S(2)}) async-start(s32[32,1,4]{2,1,0:T(1,128)} %bitcast.5), calls=%async_computation | async-start | bytes 32768 | tf_op jit(solution)/shard_map/all_to_all | solution.py:95
  23.6 1.4 reshape.154
  25.0 1.2 gather_fusion
  26.2 0.2 select_select_fusion.1
  26.4 1.2 reshape.155
  27.6 5.7 %all-to-all-done = s32[32,1,4]{2,1,0:T(1,128)S(1)} async-done(((s32[32,1,4]{2,1,0:T(1,128)}), s32[32,1,4]{2,1,0:T(1,128)S(1)}, u32[]{:S(2)}, u32[]{:S(2)}) %all-to-all-start) | async-done | bytes 544 | tf_op jit(solution)/shard_map/all_to_all | solution.py:95
  33.3 4.1 %all-to-all-start.1 = ((bf16[32,4,4096]{2,1,0:T(4,128)(2,1)}), bf16[32,4,4096]{2,1,0:T(4,128)(2,1)S(1)}, u32[]{:S(2)}, u32[]{:S(2)}) async-start(bf16[32,4,4096]{2,1,0:T(4,128)(2,1)} %reshape.155), calls=%async_computation.1 | async-start | bytes 2097152 | tf_op jit(solution)/shard_map/all_to_all | solution.py:94
  37.4 0.0 all-gather.5.cloned.1.call-start
  37.5 0.5 broadcast.131
  38.0 0.7 reduce.7
  38.7 0.1 eq.68
  38.8 0.1 select_reduce_fusion.1
  38.9 0.1 fusion.33
  39.1 28.2 %all-to-all-done.1 = bf16[32,4,4096]{2,1,0:T(4,128)(2,1)S(1)} async-done(((bf16[32,4,4096]{2,1,0:T(4,128)(2,1)}), bf16[32,4,4096]{2,1,0:T(4,128)(2,1)S(1)}, u32[]{:S(2)}, u32[]{:S(2)}) %all-to-all-start.1) | async-done | bytes 1048608 | tf_op jit(solution)/shard_map/all_to_all | solution.py:94
  67.3 0.3 reshape.156
  67.5 1.2 gather_fusion.1
  68.7 0.0 copy-start
  68.8 0.5 convert_reduce_fusion
  69.2 0.4 fusion.30
  69.7 1.5 fusion.32
  71.2 0.0 all-gather.5.cloned.1.call-update
  71.2 0.0 all-gather.9.cloned.1.call-start
  71.2 0.7 all-gather.9.cloned.1.call-update
  71.9 0.0 all-gather.11.cloned.1.call-start
  72.0 0.5 all-gather.11.cloned.1.call-update
  72.5 0.7 reduce.6
  73.2 21.6 %all-gather.7.cloned.1.call-done = bf16[4096,384]{1,0:T(8,128)(2,1)} async-done(((bf16[128,384]{1,0:T(8,128)(2,1)}), bf16[4096,384]{1,0:T(8,128)(2,1)}) %all-gather.7.cloned.1.call-update) | async-done | bytes 3145744 | tf_op jit(solution)/shard_map/all_gather | solution.py:100
  94.8 50.0 %all-gather.5.cloned.1.call-done = bf16[1024,4096]{1,0:T(8,128)(2,1)} async-done(((bf16[128,4096]{1,0:T(8,128)(2,1)}), bf16[1024,4096]{1,0:T(8,128)(2,1)}) %all-gather.5.cloned.1.call-update) | async-done | bytes 8388624 | tf_op jit(solution)/shard_map/all_gather | solution.py:98
  144.8 8.7 %multiply_convert_fusion = bf16[1024,384]{1,0:T(8,128)(2,1)S(1)} fusion(bf16[1024,4096]{1,0:T(8,128)(2,1)} %all-gather.5.cloned.1.call-done, bf16[4096,384]{1,0:T(8,128)(2,1)} %all-gather.7.cloned.1.call-done), kind=kOutput, calls=%fused_computation.33 | convolution fusion | flops 3222011904 | bytes 12320768 | tf_op jit(solution)/shard_map/dot_general | solution.py:105
  153.5 0.4 reshape.183
  154.0 0.1 copy.45
  154.1 73.7 %all-gather.9.cloned.1.call-done = bf16[4096,384]{1,0:T(8,128)(2,1)} async-done(((bf16[128,384]{1,0:T(8,128)(2,1)}), bf16[4096,384]{1,0:T(8,128)(2,1)}) %all-gather.9.cloned.1.call-update) | async-done | bytes 3145744 | tf_op jit(solution)/shard_map/all_gather | solution.py:101
  227.8 7.7 %convolution_convert_fusion.1 = bf16[1024,384]{0,1:T(8,128)(2,1)S(1)} fusion(bf16[1024,4096]{1,0:T(8,128)(2,1)} %all-gather.5.cloned.1.call-done, bf16[4096,384]{1,0:T(8,128)(2,1)} %all-gather.9.cloned.1.call-done), kind=kOutput, calls=%fused_computation.35 | convolution fusion | flops 3221618688 | bytes 12320768 | tf_op jit(solution)/shard_map/dot_general | solution.py:105
  235.5 0.4 copy.46
  235.9 70.4 %all-gather.11.cloned.1.call-done = bf16[4096,384]{1,0:T(8,128)(2,1)} async-done(((bf16[128,384]{1,0:T(8,128)(2,1)}), bf16[4096,384]{1,0:T(8,128)(2,1)}) %all-gather.11.cloned.1.call-update) | async-done | bytes 3145744 | tf_op jit(solution)/shard_map/all_gather | solution.py:102
  306.3 7.7 %convolution_convert_fusion = bf16[1024,384]{0,1:T(8,128)(2,1)S(1)} fusion(bf16[1024,4096]{1,0:T(8,128)(2,1)} %all-gather.5.cloned.1.call-done, bf16[4096,384]{1,0:T(8,128)(2,1)} %all-gather.11.cloned.1.call-done), kind=kOutput, calls=%fused_computation.34 | convolution fusion | flops 3221618688 | bytes 12320768 | tf_op jit(solution)/shard_map/dot_general | solution.py:105
  314.1 1.2 copy.47
  315.2 20.0 %while.10 = (s32[]{:T(128)}, bf16[2,512,3,128]{3,1,2,0:T(8,128)(2,1)S(1)}, s32[2,512]{1,0:T(2,128)S(1)}, s32[1,1024]{1,0:T(1,128)S(1)}, bf16[2,512,3,128]{3,1,2,...) while((s32[]{:T(128)}, ...), condition=%wide.region_12.14_spmd, body=%wide.region_9.13_spmd.sunk | while | flops 815993856 | bytes 16558177 | solution.py:113
  315.2 0.4 compare_and_fusion.4
  315.6 5.4 %fusion.58 = (f32[3,512]{1,0:T(4,128)S(1)}, f32[3,512,1024]{2,1,0:T(8,128)}) fusion(pred[512,1024]{1,0:T(8,128)(4,1)S(1)} %compare_and_fusion.4, bf16[1024,3,128]{2,0,1:T(8,128)(2,1)S(1)} %get-tuple-element.160, bf16[2,512,3,128]{3,1,2,0:T(8,128)(2,1)S(1)} %get-tuple-element.159, s32[]{:T(128)} %get-tuple-element.147), kind=kOutput, calls=%fused_computation.62.clone.1 | convolution fusion | flops 408945664 | bytes 8525828 | tf_op jit(solution)/shard_map/while/body/eval_jaxpr/sub | solution.py:67
  321.1 4.1 %fusion.59 = bf16[2,512,3,128]{3,1,2,0:T(8,128)(2,1)S(1)} fusion(bf16[2,512,3,128]{3,1,2,0:T(8,128)(2,1)S(1)} %get-tuple-element.148, s32[]{:T(128)} %get-tuple-element.147, bf16[1024,3,128]{2,0,1:T(8,128)(2,1)} %get-tuple-element.161, f32[3,512,1024]{2,1,0:T(8,128)} %get-tuple-element.137, f32[3,512]{1,0:T(4,128)S(1)} %compare_select_fusion.4), kind=kOutput, calls=%fused_computation.13.clone.1 | convolution fusion | flops 405995520 | bytes 7479300 | tf_op jit(solution)/shard_map/while/body/eval_jaxpr/hqk,khd->qhd/dot_general | solution.py:71
  325.2 0.4 compare_and_fusion.4
  325.7 5.4 %fusion.58 = (f32[3,512]{1,0:T(4,128)S(1)}, f32[3,512,1024]{2,1,0:T(8,128)}) fusion(pred[512,1024]{1,0:T(8,128)(4,1)S(1)} %compare_and_fusion.4, bf16[1024,3,128]{2,0,1:T(8,128)(2,1)S(1)} %get-tuple-element.160, bf16[2,512,3,128]{3,1,2,0:T(8,128)(2,1)S(1)} %get-tuple-element.159, s32[]{:T(128)} %get-tuple-element.147), kind=kOutput, calls=%fused_computation.62.clone.1 | convolution fusion | flops 408945664 | bytes 8525828 | tf_op jit(solution)/shard_map/while/body/eval_jaxpr/sub | solution.py:67
  331.1 4.1 %fusion.59 = bf16[2,512,3,128]{3,1,2,0:T(8,128)(2,1)S(1)} fusion(bf16[2,512,3,128]{3,1,2,0:T(8,128)(2,1)S(1)} %get-tuple-element.148, s32[]{:T(128)} %get-tuple-element.147, bf16[1024,3,128]{2,0,1:T(8,128)(2,1)} %get-tuple-element.161, f32[3,512,1024]{2,1,0:T(8,128)} %get-tuple-element.137, f32[3,512]{1,0:T(4,128)S(1)} %compare_select_fusion.4), kind=kOutput, calls=%fused_computation.13.clone.1 | convolution fusion | flops 405995520 | bytes 7479300 | tf_op jit(solution)/shard_map/while/body/eval_jaxpr/hqk,khd->qhd/dot_general | solution.py:71
  335.2 0.7 copy.52
  335.9 1.4 reshape.184
  (24 shorter events, 0.1 us)
Async XLA Ops:
  6.5 88.2 %all-gather.7.cloned.1.call-start = ((), (), s32[]{:S(2)}) async-start(), calls=%async_computation.3 | async-start | bytes 3244032 | tf_op jit(solution)/shard_map/all_gather | solution.py:100
  12.2 21.1 %all-to-all-start = ((s32[32,1,4]{2,1,0:T(1,128)}), s32[32,1,4]{2,1,0:T(1,128)S(1)}, u32[]{:S(2)}, u32[]{:S(2)}) async-start(s32[32,1,4]{2,1,0:T(1,128)} %bitcast.5), calls=%async_computation | async-start | bytes 32768 | tf_op jit(solution)/shard_map/all_to_all | solution.py:95
  26.2 11.3 %copy-start.1 = (bf16[4096]{0:T(1024)(128)(2,1)S(1)}, bf16[4096]{0:T(1024)(128)(2,1)}, u32[]{:S(2)}) copy-start(bf16[4096]{0:T(1024)(128)(2,1)} %param.18) | copy-start | bytes 24580
  33.3 34.0 %all-to-all-start.1 = ((bf16[32,4,4096]{2,1,0:T(4,128)(2,1)}), bf16[32,4,4096]{2,1,0:T(4,128)(2,1)S(1)}, u32[]{:S(2)}, u32[]{:S(2)}) async-start(bf16[32,4,4096]{2,1,0:T(4,128)(2,1)} %reshape.155), calls=%async_computation.1 | async-start | bytes 2097152 | tf_op jit(solution)/shard_map/all_to_all | solution.py:94
  37.4 107.4 %all-gather.5.cloned.1.call-start = ((), (), s32[]{:S(2)}) async-start(), calls=%async_computation.2 | async-start | bytes 9437184 | tf_op jit(solution)/shard_map/all_gather | solution.py:98
  68.7 3.8 %copy-start = (s32[1,1024]{1,0:T(1,128)S(1)}, s32[1,1024]{1,0:T(1,128)}, u32[]{:S(2)}) copy-start(s32[1,1024]{1,0:T(1,128)} %param.17) | copy-start | bytes 12292
  71.2 156.6 %all-gather.9.cloned.1.call-start = ((), (), s32[]{:S(2)}) async-start(), calls=%async_computation.4 | async-start | bytes 3244032 | tf_op jit(solution)/shard_map/all_gather | solution.py:101
  71.9 234.4 %all-gather.11.cloned.1.call-start = ((), (), s32[]{:S(2)}) async-start(), calls=%async_computation.5 | async-start | bytes 3244032 | tf_op jit(solution)/shard_map/all_gather | solution.py:102
Sparse Core Ops, SparseCore 0:
  9.9 84.8 all-gather.6
  96.6 48.1 all-gather.4
  147.4 80.3 all-gather.8
  230.2 76.0 all-gather.10
where the time goes:
time: 344 us
  waiting for transfers between devices  252 us (73%)
  matrix products  43.3 us (13%)
  starting transfers between devices  15.5 us (5%)
  between operations  13.4 us (4%)
  local copies, waits for them, and re-layouts  12.3 us (4%)
  other arithmetic  7.78 us (2%)
    all_gather x1, waiting for transfers between devices, body(): lax.all_gather(w_key, 'dp', axis=0, tiled=True)  73.7 us
    all_gather x1, waiting for transfers between devices, body(): lax.all_gather(w_value, 'dp', axis=0, tiled=True)  70.4 us
    all_gather x1, waiting for transfers between devices, body(): normed_row = lax.all_gather(normed_own, 'tensor', axis=0, tiled=True)  50 us
    all_to_all x1, waiting for transfers between devices, body(): lax.all_to_all(send_rows, 'dp', split_axis=0, concat_axis=0, tiled=True)  28.2 us
    dot_general x3, matrix products, body(): jnp.dot(normed_row, piece_w, preferred_element_type=jnp.float32)  24.2 us
    all_gather x1, waiting for transfers between devices, body(): lax.all_gather(w_query, 'dp', axis=0, tiled=True)  21.6 us
    all_to_all x1, starting transfers between devices, body(): lax.all_to_all(send_slots, 'dp', split_axis=0, concat_axis=0, tiled=True)  11.3 us
    sub x2, matrix products, attend(): weights = jnp.where(allowed[None], jnp.exp(masked - largest), 0.0)  10.8 us
  transfers between devices with their start and end apart: 6, of which 6 were waited for; matrix products, arithmetic and copies ran while one was open for 9% of the time, Pallas kernels for 0%

commit v1 on v0

--- a/solution.py
+++ b/solution.py
@@ -5,6 +5,13 @@
 
 HS = 128
 block_rows = 512
+
+
+def gather_over(block, mesh_axis, dim):
+    size = lax.axis_size(mesh_axis)
+    shards = jnp.stack([block for _ in range(size)])
+    shards = lax.all_to_all(shards, mesh_axis, split_axis=0, concat_axis=0)
+    return jnp.concatenate(shards, axis=dim)
 
 
 def layer_norm(values_in, ln_gain):
@@ -97,7 +104,7 @@
     normed_own = layer_norm(place_rows(recv_rows, recv_slots, tok_rows), ln_gain)
     normed_row = lax.all_gather(normed_own, "tensor", axis=0, tiled=True)
     pieces_in = (
-        lax.all_gather(w_query, "dp", axis=0, tiled=True),
+        gather_over(w_query, "dp", 0),
         lax.all_gather(w_key, "dp", axis=0, tiled=True),
         lax.all_gather(w_value, "dp", axis=0, tiled=True),
     )

time: 344 us -> 322 us (0.936)
  waiting for transfers between devices: 252 us -> 221 us
  starting transfers between devices: 15.5 us -> 20.8 us
  local copies, waits for them, and re-layouts: 12.3 us -> 16.3 us
    all_to_all x0 -> x1, waiting for transfers between devices: none -> 74.2 us  [gather_over(): shards = lax.all_to_all(shards, mesh_axis, split_axis=0, concat_axis=0)]
    all_gather x1, waiting for transfers between devices: 50 us -> 0.01 us  [body(): normed_row = lax.all_gather(normed_own, 'tensor', axis=0, tiled=True)]
    all_gather x1, waiting for transfers between devices: 73.7 us -> 42.7 us  [body(): lax.all_gather(w_key, 'dp', axis=0, tiled=True)]
    all_gather x1 -> x0, waiting for transfers between devices: 21.6 us -> none  [body(): lax.all_gather(w_query, 'dp', axis=0, tiled=True)]
    all_to_all x0 -> x1, starting transfers between devices: none -> 5.06 us  [gather_over(): shards = lax.all_to_all(shards, mesh_axis, split_axis=0, concat_axis=0)]
  transfers between devices with their start and end apart: 6 -> 6, of which waited for: 6 -> 5; matrix products, arithmetic and copies ran while one was open for 9% -> 8% of each run, Pallas kernels for 0% -> 0%
where the time goes in v1:
time: 322 us
  waiting for transfers between devices  221 us (69%)
  matrix products  42.3 us (13%)
  starting transfers between devices  20.8 us (6%)
  local copies, waits for them, and re-layouts  16.3 us (5%)
  between operations  13.4 us (4%)
  other arithmetic  7.72 us (2%)
    all_to_all x1, waiting for transfers between devices, gather_over(): shards = lax.all_to_all(shards, mesh_axis, split_axis=0, concat_axis=0)  74.2 us
    all_gather x1, waiting for transfers between devices, body(): lax.all_gather(w_value, 'dp', axis=0, tiled=True)  70.6 us
    all_gather x1, waiting for transfers between devices, body(): lax.all_gather(w_key, 'dp', axis=0, tiled=True)  42.7 us
    all_to_all x1, waiting for transfers between devices, body(): lax.all_to_all(send_rows, 'dp', split_axis=0, concat_axis=0, tiled=True)  26.6 us
    dot_general x3, matrix products, body(): jnp.dot(normed_row, piece_w, preferred_element_type=jnp.float32)  23.3 us
    all_to_all x1, starting transfers between devices, body(): lax.all_to_all(send_slots, 'dp', split_axis=0, concat_axis=0, tiled=True)  11.3 us
    sub x2, matrix products, attend(): weights = jnp.where(allowed[None], jnp.exp(masked - largest), 0.0)  10.8 us
    dot_general x2, matrix products, attend(): jnp.einsum('hqk,khd->qhd', weights_bf, value_rows, preferred_element_type...  8.16 us
  transfers between devices with their start and end apart: 6, of which 5 were waited for; matrix products, arithmetic and copies ran while one was open for 8% of the time, Pallas kernels for 0%

profile of v1, /device:TPU:8, one launch (start us, length us, event | category | flops | bytes accessed | tf_op | source)
XLA Modules:
  0.0 321.6 jit_solution(9422289802705823007)
XLA Ops:
  6.5 0.8 copy.40
  7.3 0.1 reshape.158
  7.4 0.1 fusion.35
  7.5 0.2 reduce_window_sum.11
  7.7 0.2 select_reduce_fusion.4
  7.9 0.7 broadcast_compare_fusion.1
  8.5 0.1 copy.39
  8.7 0.1 reshape.157
  8.8 0.7 maximum_add_fusion
  9.5 0.1 copy.43
  9.6 0.1 broadcast_in_dim.112
  9.7 0.7 broadcast_subtract_fusion
  10.3 0.1 copy.41
  10.4 0.1 broadcast_in_dim.107
  10.6 0.1 fusion.34
  10.7 0.1 select_reduce_fusion.3
  10.8 0.7 select_n.65
  11.5 11.3 %all-to-all-start = ((s32[32,1,4]{2,1,0:T(1,128)}), s32[32,1,4]{2,1,0:T(1,128)S(1)}, u32[]{:S(2)}, u32[]{:S(2)}) async-start(s32[32,1,4]{2,1,0:T(1,128)} %bitcast.5), calls=%async_computation | async-start | bytes 32768 | tf_op jit(solution)/shard_map/all_to_all | solution.py:102
  22.9 1.3 reshape.159
  24.2 1.2 gather_fusion
  25.4 0.0 copy-start.3
  25.4 0.2 select_select_fusion.1
  25.7 1.2 reshape.160
  26.9 5.7 %all-to-all-done = s32[32,1,4]{2,1,0:T(1,128)S(1)} async-done(((s32[32,1,4]{2,1,0:T(1,128)}), s32[32,1,4]{2,1,0:T(1,128)S(1)}, u32[]{:S(2)}, u32[]{:S(2)}) %all-to-all-start) | async-done | bytes 544 | tf_op jit(solution)/shard_map/all_to_all | solution.py:102
  32.6 4.1 %all-to-all-start.1 = ((bf16[32,4,4096]{2,1,0:T(4,128)(2,1)}), bf16[32,4,4096]{2,1,0:T(4,128)(2,1)S(1)}, u32[]{:S(2)}, u32[]{:S(2)}) async-start(bf16[32,4,4096]{2,1,0:T(4,128)(2,1)} %reshape.160), calls=%async_computation.1 | async-start | bytes 2097152 | tf_op jit(solution)/shard_map/all_to_all | solution.py:101
  36.7 0.0 all-gather.4.cloned.1.call-start
  36.8 0.5 broadcast.133
  37.3 0.7 reduce.7
  37.9 0.1 eq.68
  38.0 0.1 select_reduce_fusion.1
  38.2 0.1 fusion.33
  38.3 26.6 %all-to-all-done.1 = bf16[32,4,4096]{2,1,0:T(4,128)(2,1)S(1)} async-done(((bf16[32,4,4096]{2,1,0:T(4,128)(2,1)}), bf16[32,4,4096]{2,1,0:T(4,128)(2,1)S(1)}, u32[]{:S(2)}, u32[]{:S(2)}) %all-to-all-start.1) | async-done | bytes 1048608 | tf_op jit(solution)/shard_map/all_to_all | solution.py:101
  64.9 0.3 reshape.161
  65.2 1.2 gather_fusion.1
  66.4 0.5 convert_reduce_fusion
  66.9 0.4 fusion.30
  67.3 1.5 fusion.32
  68.8 0.0 all-gather.4.cloned.1.call-update
  68.8 0.0 all-gather.6.cloned.1.call-start
  68.9 0.7 all-gather.6.cloned.1.call-update
  69.6 2.1 stack.2
  71.7 5.1 %all-to-all-start.2 = ((bf16[32,128,384]{2,1,0:T(8,128)(2,1)}), bf16[32,128,384]{2,1,0:T(8,128)(2,1)S(1)}, u32[]{:S(2)}, u32[]{:S(2)}) async-start(bf16[32,128,384]{2,1,0:T(8,128)(2,1)} %stack.2), calls=%async_computation.2 | async-start | bytes 6291456 | tf_op jit(solution)/shard_map/all_to_all | solution.py:13
  76.8 0.2 all-gather.8.cloned.1.call-start
  77.0 0.5 all-gather.8.cloned.1.call-update
  77.5 0.6 reduce.6
  78.2 74.2 %all-to-all-done.2 = bf16[32,128,384]{2,1,0:T(8,128)(2,1)S(1)} async-done(((bf16[32,128,384]{2,1,0:T(8,128)(2,1)}), bf16[32,128,384]{2,1,0:T(8,128)(2,1)S(1)}, u32[]{:S(2)}, u32[]{:S(2)}) %all-to-all-start.2) | async-done | bytes 3145760 | tf_op jit(solution)/shard_map/all_to_all | solution.py:13
  152.3 7.9 %multiply_convert_fusion = bf16[1024,384]{1,0:T(8,128)(2,1)} fusion(bf16[1024,4096]{1,0:T(8,128)(2,1)} %all-gather.4.cloned.1.call-done, bf16[4096,384]{1,0:T(8,128)(2,1)S(1)} %bitcast.46), kind=kOutput, calls=%fused_computation.33 | convolution fusion | flops 3222011904 | bytes 12320768 | tf_op jit(solution)/shard_map/dot_general | solution.py:112
  160.2 2.4 reshape.189
  162.6 0.1 copy.45
  162.7 42.7 %all-gather.6.cloned.1.call-done = bf16[4096,384]{1,0:T(8,128)(2,1)} async-done(((bf16[128,384]{1,0:T(8,128)(2,1)}), bf16[4096,384]{1,0:T(8,128)(2,1)}) %all-gather.6.cloned.1.call-update) | async-done | bytes 3145744 | tf_op jit(solution)/shard_map/all_gather | solution.py:108
  205.4 7.7 %convolution_convert_fusion.1 = bf16[1024,384]{0,1:T(8,128)(2,1)S(1)} fusion(bf16[1024,4096]{1,0:T(8,128)(2,1)} %all-gather.4.cloned.1.call-done, bf16[4096,384]{1,0:T(8,128)(2,1)} %all-gather.6.cloned.1.call-done), kind=kOutput, calls=%fused_computation.35 | convolution fusion | flops 3221618688 | bytes 12320768 | tf_op jit(solution)/shard_map/dot_general | solution.py:112
  213.1 0.4 copy.46
  213.5 70.6 %all-gather.8.cloned.1.call-done = bf16[4096,384]{1,0:T(8,128)(2,1)} async-done(((bf16[128,384]{1,0:T(8,128)(2,1)}), bf16[4096,384]{1,0:T(8,128)(2,1)}) %all-gather.8.cloned.1.call-update) | async-done | bytes 3145744 | tf_op jit(solution)/shard_map/all_gather | solution.py:109
  284.1 7.7 %convolution_convert_fusion = bf16[1024,384]{0,1:T(8,128)(2,1)S(1)} fusion(bf16[1024,4096]{1,0:T(8,128)(2,1)} %all-gather.4.cloned.1.call-done, bf16[4096,384]{1,0:T(8,128)(2,1)} %all-gather.8.cloned.1.call-done), kind=kOutput, calls=%fused_computation.34 | convolution fusion | flops 3221618688 | bytes 12320768 | tf_op jit(solution)/shard_map/dot_general | solution.py:112
  291.8 1.2 copy.47
  293.0 19.9 %while.10 = (s32[]{:T(128)}, bf16[2,512,3,128]{3,1,2,0:T(8,128)(2,1)S(1)}, s32[2,512]{1,0:T(2,128)S(1)}, s32[1,1024]{1,0:T(1,128)S(1)}, bf16[2,512,3,128]{3,1,2,...) while((s32[]{:T(128)}, ...), condition=%wide.region_12.14_spmd, body=%wide.region_9.13_spmd.sunk | while | flops 815993856 | bytes 16558177 | solution.py:120
  293.0 0.4 compare_and_fusion.4
  293.4 5.4 %fusion.58 = (f32[3,512]{1,0:T(4,128)S(1)}, f32[3,512,1024]{2,1,0:T(8,128)}) fusion(pred[512,1024]{1,0:T(8,128)(4,1)S(1)} %compare_and_fusion.4, bf16[1024,3,128]{2,0,1:T(8,128)(2,1)S(1)} %get-tuple-element.160, bf16[2,512,3,128]{3,1,2,0:T(8,128)(2,1)S(1)} %get-tuple-element.159, s32[]{:T(128)} %get-tuple-element.147), kind=kOutput, calls=%fused_computation.62.clone.1 | convolution fusion | flops 408945664 | bytes 8525828 | tf_op jit(solution)/shard_map/while/body/eval_jaxpr/sub | solution.py:74
  298.9 4.1 %fusion.59 = bf16[2,512,3,128]{3,1,2,0:T(8,128)(2,1)S(1)} fusion(bf16[2,512,3,128]{3,1,2,0:T(8,128)(2,1)S(1)} %get-tuple-element.148, s32[]{:T(128)} %get-tuple-element.147, bf16[1024,3,128]{2,0,1:T(8,128)(2,1)} %get-tuple-element.161, f32[3,512,1024]{2,1,0:T(8,128)} %get-tuple-element.137, f32[3,512]{1,0:T(4,128)S(1)} %compare_select_fusion.4), kind=kOutput, calls=%fused_computation.13.clone.1 | convolution fusion | flops 405995520 | bytes 7479300 | tf_op jit(solution)/shard_map/while/body/eval_jaxpr/hqk,khd->qhd/dot_general | solution.py:78
  303.0 0.4 compare_and_fusion.4
  303.4 5.4 %fusion.58 = (f32[3,512]{1,0:T(4,128)S(1)}, f32[3,512,1024]{2,1,0:T(8,128)}) fusion(pred[512,1024]{1,0:T(8,128)(4,1)S(1)} %compare_and_fusion.4, bf16[1024,3,128]{2,0,1:T(8,128)(2,1)S(1)} %get-tuple-element.160, bf16[2,512,3,128]{3,1,2,0:T(8,128)(2,1)S(1)} %get-tuple-element.159, s32[]{:T(128)} %get-tuple-element.147), kind=kOutput, calls=%fused_computation.62.clone.1 | convolution fusion | flops 408945664 | bytes 8525828 | tf_op jit(solution)/shard_map/while/body/eval_jaxpr/sub | solution.py:74
  308.8 4.1 %fusion.59 = bf16[2,512,3,128]{3,1,2,0:T(8,128)(2,1)S(1)} fusion(bf16[2,512,3,128]{3,1,2,0:T(8,128)(2,1)S(1)} %get-tuple-element.148, s32[]{:T(128)} %get-tuple-element.147, bf16[1024,3,128]{2,0,1:T(8,128)(2,1)} %get-tuple-element.161, f32[3,512,1024]{2,1,0:T(8,128)} %get-tuple-element.137, f32[3,512]{1,0:T(4,128)S(1)} %compare_select_fusion.4), kind=kOutput, calls=%fused_computation.13.clone.1 | convolution fusion | flops 405995520 | bytes 7479300 | tf_op jit(solution)/shard_map/while/body/eval_jaxpr/hqk,khd->qhd/dot_general | solution.py:78
  312.9 0.7 copy.52
  313.6 1.4 reshape.190
  (28 shorter events, 0.1 us)
Async XLA Ops:
  11.5 21.1 %all-to-all-start = ((s32[32,1,4]{2,1,0:T(1,128)}), s32[32,1,4]{2,1,0:T(1,128)S(1)}, u32[]{:S(2)}, u32[]{:S(2)}) async-start(s32[32,1,4]{2,1,0:T(1,128)} %bitcast.5), calls=%async_computation | async-start | bytes 32768 | tf_op jit(solution)/shard_map/all_to_all | solution.py:102
  25.4 11.3 %copy-start.3 = (bf16[4096]{0:T(1024)(128)(2,1)S(1)}, bf16[4096]{0:T(1024)(128)(2,1)}, u32[]{:S(2)}) copy-start(bf16[4096]{0:T(1024)(128)(2,1)} %param.18) | copy-start | bytes 24580
  32.6 32.3 %all-to-all-start.1 = ((bf16[32,4,4096]{2,1,0:T(4,128)(2,1)}), bf16[32,4,4096]{2,1,0:T(4,128)(2,1)S(1)}, u32[]{:S(2)}, u32[]{:S(2)}) async-start(bf16[32,4,4096]{2,1,0:T(4,128)(2,1)} %reshape.160), calls=%async_computation.1 | async-start | bytes 2097152 | tf_op jit(solution)/shard_map/all_to_all | solution.py:101
  36.7 115.6 %all-gather.4.cloned.1.call-start = ((), (), s32[]{:S(2)}) async-start(), calls=%async_computation.3 | async-start | bytes 9437184 | tf_op jit(solution)/shard_map/all_gather | solution.py:105
  66.4 3.2 copy-start.2
  68.8 136.6 %all-gather.6.cloned.1.call-start = ((), (), s32[]{:S(2)}) async-start(), calls=%async_computation.4 | async-start | bytes 3244032 | tf_op jit(solution)/shard_map/all_gather | solution.py:108
  71.7 5.8 %copy-start.1 = (s32[1,1024]{1,0:T(1,128)S(1)}, s32[1,1024]{1,0:T(1,128)}, u32[]{:S(2)}) copy-start(s32[1,1024]{1,0:T(1,128)} %param.17) | copy-start | bytes 12292
  71.7 80.6 %all-to-all-start.2 = ((bf16[32,128,384]{2,1,0:T(8,128)(2,1)}), bf16[32,128,384]{2,1,0:T(8,128)(2,1)S(1)}, u32[]{:S(2)}, u32[]{:S(2)}) async-start(bf16[32,128,384]{2,1,0:T(8,128)(2,1)} %stack.2), calls=%async_computation.2 | async-start | bytes 6291456 | tf_op jit(solution)/shard_map/all_to_all | solution.py:13
  76.8 207.3 %all-gather.8.cloned.1.call-start = ((), (), s32[]{:S(2)}) async-start(), calls=%async_computation.5 | async-start | bytes 3244032 | tf_op jit(solution)/shard_map/all_gather | solution.py:109
  213.5 79.5 %copy-start = (bf16[2,512,3,128]{3,1,2,0:T(8,128)(2,1)S(1)}, bf16[2,512,3,128]{3,1,2,0:T(8,128)(2,1)}, u32[]{:S(2)}) copy-start(bf16[2,512,3,128]{3,1,2,0:T(8,128)(2,1)} %custom-call.4) | copy-start | bytes 2359300
Sparse Core Ops, SparseCore 0:
  68.9 47.8 all-gather.3
  119.5 85.8 all-gather.5
  208.0 76.0 all-gather.7
